TPU v7x, 512 devices: a whole 4x8x8 slice. The times are simulated.
512 devices in a mesh: ctx: 256 (over z, y, x), head: 2 (over core).
Axes of the slice: x: 4, y: 8, z: 8, core: 2. Of those that a mesh axis runs over, the one named last changes fastest.
Arguments:
- queries: bfloat16 [65536, 8192], P(('ctx', 'head')), may hold values from -64 to 64
- keys: bfloat16 [65536, 1024], P(('ctx', 'head')), may hold values from -64 to 64
- values: bfloat16 [65536, 1024], P(('ctx', 'head')), may hold values from -6 to 6
- doc_lengths: int32 [192], replicated, may hold values from 1 to 1024, as said below
Outputs:
- attended: bfloat16 [65536, 8192], P(('ctx', 'head'))
Inputs may be any that keep to these rules, and one draw needn't show every extreme that they name: `doc_lengths`: the lengths sum to 65536; the first document has one token, the second exactly 1024, and no other more than 1024.
All inputs are finite; a program needn't handle non-finite values.
Results may differ from a plain program's by a relative error of at most 0.004.
Values may be sent and summed in bfloat16 or wider, within the bound.
A program may use at most 64 MiB of HBM per device.

v0:
```python
import jax
import jax.numpy as jnp
from jax import lax
from jax.sharding import PartitionSpec as P

H = 64
KVH = 8
HD = 128
REACH = 4


def from_behind(block, axis, distance):
    devices = range(lax.axis_size(axis))
    route = [(i - distance, i) for i in devices if i - distance in devices]
    return lax.ppermute(block, axis, route)


def doc_index(positions, doc_ends):
    return jnp.sum((doc_ends[None, :] <= positions[:, None]).astype(jnp.int32), axis=1)


def per_device(queries, keys, values, doc_lengths):
    group_size = H // KVH
    score_scale = HD ** (-0.5)
    doc_ends = jnp.cumsum(doc_lengths)
    my_span = lax.axis_index("ctx")
    local_queries, local_keys, local_values = (
        lax.all_to_all(queries, "head", split_axis=1, concat_axis=0, tiled=True),
        lax.all_to_all(keys, "head", split_axis=1, concat_axis=0, tiled=True),
        lax.all_to_all(values, "head", split_axis=1, concat_axis=0, tiled=True),
    )
    first_row = my_span * local_queries.shape[0]
    kv_own = jnp.stack((local_keys, local_values))
    span_rows = kv_own.shape[1]
    query_count = local_queries.shape[0]
    kv_heads = kv_own.shape[2] // HD
    query_rows = min(256, query_count)
    query_blocked = local_queries.reshape(query_count, kv_heads, group_size, HD)
    query_pos = first_row + jnp.arange(query_count, dtype=jnp.int32)
    query_doc = doc_index(query_pos, doc_ends)
    running = (
        jnp.full((query_count, kv_heads, group_size), -1e30, jnp.float32),
        jnp.zeros((query_count, kv_heads, group_size), jnp.float32),
        jnp.zeros((query_count, kv_heads, group_size, HD), jnp.float32),
    )

    def absorb(running, kv_pair, source):
        key_rows = kv_pair[0].reshape(span_rows, kv_heads, HD)
        value_rows = kv_pair[1].reshape(span_rows, kv_heads, HD)
        key_pos = source * span_rows + jnp.arange(span_rows, dtype=jnp.int32)
        key_doc = doc_index(key_pos, doc_ends)
        key_live = key_pos >= 0

        def one_block(block_index, current):
            allowed = (
                (query_doc[:, None] == key_doc[None, :])
                & (key_pos[None, :] <= query_pos[:, None])
                & key_live[None, :]
            )

            def update_tile(state):
                row_max, row_sum, weighted = state
                scores = (
                    jnp.einsum(
                        "qkgd,skd->qkgs",
                        query_blocked,
                        key_rows,
                        preferred_element_type=jnp.float32,
                    )
                    * score_scale
                )
                wide = allowed[:, None, None, :]
                max_new = jnp.maximum(
                    row_max, jnp.max(jnp.where(wide, scores, jnp.float32(-1e30)), axis=-1)
                )
                weights = jnp.where(wide, jnp.exp(scores - max_new[..., None]), jnp.float32(0.0))
                rescale = jnp.exp(row_max - max_new)
                sum_new = row_sum * rescale + jnp.sum(weights, axis=-1)
                acc_new = weighted * rescale[..., None] + jnp.einsum(
                    "qkgs,skd->qkgd",
                    weights.astype(jnp.bfloat16),
                    value_rows,
                    preferred_element_type=jnp.float32,
                )
                return (max_new, sum_new, acc_new)

            return lax.cond(jnp.any(allowed), update_tile, lambda state: state, current)

        return lax.fori_loop(0, query_count // query_rows, one_block, running)

    running = absorb(running, kv_own, my_span)
    moving = kv_own
    for distance in range(1, REACH + 1):
        moving = from_behind(moving, "ctx", 1)
        running = absorb(running, moving, my_span - distance)
    row_max, row_sum, weighted = running
    finished = (
        (weighted / row_sum[..., None])
        .astype(jnp.bfloat16)
        .reshape(query_count, kv_heads * group_size * HD)
    )
    return lax.all_to_all(finished, "head", split_axis=0, concat_axis=1, tiled=True)


def solution(mesh):
    placed = (P(("ctx", "head"), None), P(("ctx", "head"), None), P(("ctx", "head"), None), P())
    return jax.shard_map(
        per_device, mesh=mesh, in_specs=placed, out_specs=P(("ctx", "head"), None), check_vma=False
    )
```

profile of v0, /device:TPU:256, one launch (start us, length us, event | category | flops | bytes accessed | tf_op | source)
XLA Modules:
  0.0 164.1 jit_solution(9833209813830603747)
XLA Ops:
  0.0 1.7 %copy.169 = bf16[16,2,8,512]{3,2,0,1:T(8,128)(2,1)} copy(bf16[16,2,8,512]{3,2,1,0:T(8,128)(2,1)} %bitcast.200) | data formatting | bytes 524288 | tf_op jit(solution)/shard_map/all_to_all | solution.py:30
  1.7 3.4 %all-to-all-start.2 = ((bf16[128,2,512]{2,0,1:T(8,128)(2,1)}), bf16[128,2,512]{2,0,1:T(8,128)(2,1)S(1)}, u32[]{:S(2)}, u32[]{:S(2)}) async-start(bf16[128,2,512]{2,0,1:T(8,128)(2,1)} %bitcast.173), calls=%async_computation.2 | async-start | bytes 524288 | tf_op jit(solution)/shard_map/all_to_all | solution.py:30
  5.1 1.7 %copy.170 = bf16[16,2,8,512]{3,2,0,1:T(8,128)(2,1)} copy(bf16[16,2,8,512]{3,2,1,0:T(8,128)(2,1)} %bitcast.201) | data formatting | bytes 524288 | tf_op jit(solution)/shard_map/all_to_all | solution.py:29
  6.8 0.0 all-to-all-done.2
  6.8 3.4 %all-to-all-start = ((bf16[128,2,512]{2,0,1:T(8,128)(2,1)}), bf16[128,2,512]{2,0,1:T(8,128)(2,1)S(1)}, u32[]{:S(2)}, u32[]{:S(2)}) async-start(bf16[128,2,512]{2,0,1:T(8,128)(2,1)} %bitcast.174), calls=%async_computation | async-start | bytes 524288 | tf_op jit(solution)/shard_map/all_to_all | solution.py:29
  10.3 0.1 copy.134
  10.4 1.4 all-to-all-done
  11.8 0.1 copy.133
  11.9 0.8 pad_maximum_fusion
  12.8 3.4 %collective-permute-start = (bf16[2,256,512]{1,2,0:T(8,128)(2,1)}, bf16[2,256,512]{1,2,0:T(8,128)(2,1)S(1)}, u32[]{:S(2)}, u32[]{:S(2)}) collective-permute-start(bf16[2,256,512]{1,2,0:T(8,128)(2,1)} %pad_maximum_fusion), channel_id=1, source_target_pairs={{0,2},{2,4},{4,6},{6,8},{8,10},{10,12},{12,14},{14,16},{16,18},{18... | collective-permute-start | bytes 1572872 | tf_op jit(solution)/shard_map/ppermute | solution.py:15
  16.2 3.1 %copy.168 = bf16[16,2,8,4096]{3,2,0,1:T(8,128)(2,1)} copy(bf16[16,2,8,4096]{3,2,1,0:T(8,128)(2,1)} %bitcast.189) | data formatting | bytes 4194304 | tf_op jit(solution)/shard_map/all_to_all | solution.py:28
  19.3 3.8 %all-to-all-start.1 = ((bf16[128,2,4096]{2,0,1:T(8,128)(2,1)}), bf16[128,2,4096]{2,0,1:T(8,128)(2,1)S(1)}, u32[]{:S(2)}, u32[]{:S(2)}) async-start(bf16[128,2,4096]{2,0,1:T(8,128)(2,1)} %bitcast.182), calls=%async_computation.1 | async-start | bytes 4194304 | tf_op jit(solution)/shard_map/all_to_all | solution.py:28
  23.1 0.0 copy-done.3
  23.1 0.3 reduce-window.9
  23.4 0.1 slice.38
  23.5 10.7 %collective-permute-done = bf16[2,256,512]{1,2,0:T(8,128)(2,1)S(1)} collective-permute-done((bf16[2,256,512]{1,2,0:T(8,128)(2,1)}, bf16[2,256,512]{1,2,0:T(8,128)(2,1)S(1)}, u32[]{:S(2)}, u32[]{:S(2)}) %collective-permute-start) | collective-permute-done | bytes 524320 | tf_op jit(solution)/shard_map/ppermute | solution.py:15
  34.3 1.9 %collective-permute-start.1 = (bf16[2,256,512]{1,2,0:T(8,128)(2,1)S(1)}, bf16[2,256,512]{1,2,0:T(8,128)(2,1)S(1)}, u32[]{:S(2)}, u32[]{:S(2)}) collective-permute-start(bf16[2,256,512]{1,2,0:T(8,128)(2,1)S(1)} %collective-permute-done), channel_id=1, source_target_pairs={{0,2},{2,4},{4,6},{6,8},{8,10},{10,12},{12,14},{14,16},{16,18},{18... | collective-permute-start | bytes 1572872 | tf_op jit(solution)/shard_map/ppermute | solution.py:15
  36.3 18.4 %collective-permute-done.1 = bf16[2,256,512]{1,2,0:T(8,128)(2,1)S(1)} collective-permute-done((bf16[2,256,512]{1,2,0:T(8,128)(2,1)S(1)}, bf16[2,256,512]{1,2,0:T(8,128)(2,1)S(1)}, u32[]{:S(2)}, u32[]{:S(2)}) %collective-permute-start.1) | collective-permute-done | bytes 524320 | tf_op jit(solution)/shard_map/ppermute | solution.py:15
  54.7 1.9 %collective-permute-start.2 = (bf16[2,256,512]{1,2,0:T(8,128)(2,1)S(1)}, bf16[2,256,512]{1,2,0:T(8,128)(2,1)}, u32[]{:S(2)}, u32[]{:S(2)}) collective-permute-start(bf16[2,256,512]{1,2,0:T(8,128)(2,1)S(1)} %collective-permute-done.1), channel_id=1, source_target_pairs={{0,2},{2,4},{4,6},{6,8},{8,10},{10,12},{12,14},{14,16},{16,18},{18... | collective-permute-start | bytes 1572872 | tf_op jit(solution)/shard_map/ppermute | solution.py:15
  56.6 0.1 slice_reduce_fusion
  56.8 0.1 add_bitcast_fusion
  56.8 0.2 convert_reduce_fusion
  57.0 17.4 %collective-permute-done.2 = bf16[2,256,512]{1,2,0:T(8,128)(2,1)} collective-permute-done((bf16[2,256,512]{1,2,0:T(8,128)(2,1)S(1)}, bf16[2,256,512]{1,2,0:T(8,128)(2,1)}, u32[]{:S(2)}, u32[]{:S(2)}) %collective-permute-start.2) | collective-permute-done | bytes 524320 | tf_op jit(solution)/shard_map/ppermute | solution.py:15
  74.4 1.9 %collective-permute-start.3 = (bf16[2,256,512]{1,2,0:T(8,128)(2,1)}, bf16[2,256,512]{1,2,0:T(8,128)(2,1)}, u32[]{:S(2)}, u32[]{:S(2)}) collective-permute-start(bf16[2,256,512]{1,2,0:T(8,128)(2,1)} %collective-permute-done.2), channel_id=1, source_target_pairs={{0,2},{2,4},{4,6},{6,8},{8,10},{10,12},{12,14},{14,16},{16,18},{18... | collective-permute-start | bytes 1572872 | tf_op jit(solution)/shard_map/ppermute | solution.py:15
  76.3 0.0 copy-done.1
  76.3 1.5 and_and_fusion
  80.9 0.1 reshape_squeeze_stack.6
  81.0 0.0 all-to-all-done.1
  81.0 0.0 copy-start
  81.0 1.3 copy-done
  82.3 2.1 %copy.138 = bf16[32,8,32,128]{3,2,1,0:T(8,128)(2,1)S(1)} copy(bf16[32,8,32,128]{3,1,2,0:T(8,128)(2,1)} %bitcast.181) | data formatting | bytes 4194304
  84.4 0.1 reshape_squeeze_stack.7
  84.5 2.4 %broadcast_in_dim.166 = f32[256,4,8,128]{3,0,2,1:T(8,128)} broadcast(f32[]{:T(128)} %constant.103.clone.1), dimensions={} | broadcast | bytes 4194308 | tf_op jit(solution)/shard_map/broadcast_in_dim | solution.py:44
  86.9 10.6 %conditional.5 = ((f32[256,4,8]{0,2,1:T(8,128)S(1)}, f32[256,4,8]{0,2,1:T(8,128)S(1)}, f32[256,4,8,128]{3,0,2,1:T(8,128)})) conditional(s32[]{:T(128)} %convert_element_type.65, (f32[256,4,8]{0,2,1:T(8,128)S(1)}, f32[256,4,8]{0,2,1:T(8,128)S(1)}, f32[256,4,8,128]{3,0,2,1:T(8,128)}) %tuple.55, (pred[256,256]{0,1:T(8,128)(4,1)S(1)}, ...), branch_computations={%region_12.13_spmd, %region_13.0_spmd} | conditional | flops 1098924032 | bytes 36896800 | solution.py:87
  86.9 2.3 %fusion = (f32[256,4,8]{0,2,1:T(8,128)S(1)}, f32[4,256,256,8]{2,1,3,0:T(8,128)S(1)}) fusion(pred[256,256]{0,1:T(8,128)(4,1)S(1)} %get-tuple-element.317, bf16[256,4,8,128]{3,2,1,0:T(8,128)(2,1)S(1)} %get-tuple-element.473, bf16[256,4,128,1]{2,1,0,3:T(4,128)(2,1)S(1)} %bitcast.190), kind=kOutput, calls=%fused_computation.2 | convolution fusion | flops 543154176 | bytes 10846208 | tf_op jit(solution)/shard_map/while/body/eval_jaxpr/cond/branch_1_fun/qkgd,skd->qkgs/dot_general | solution.py:64
  89.2 1.8 %fusion.4 = f32[256,4,8]{0,2,1:T(8,128)S(1)} fusion(f32[4,256,256,8]{2,1,3,0:T(8,128)S(1)} %get-tuple-element.528, f32[256,4,8]{0,2,1:T(8,128)S(1)} %max.11, pred[256,256]{0,1:T(8,128)(4,1)S(1)} %get-tuple-element.317), kind=kLoop, calls=%fused_computation.6 | loop fusion | flops 8380416 | bytes 8519680 | tf_op jit(solution)/shard_map/while/body/eval_jaxpr/cond/branch_1_fun/reduce_sum | solution.py:78
  91.1 6.4 %bitcast_add_fusion = f32[256,4,8,128]{3,0,2,1:T(8,128)} fusion(f32[256,4,8,128]{3,0,2,1:T(8,128)} %get-tuple-element.321, f32[256,4,8]{0,2,1:T(8,128)S(1)} %get-tuple-element.510, f32[4,256,256,8]{2,1,3,0:T(8,128)S(1)} %get-tuple-element.528, f32[256,4,8]{0,2,1:T(8,128)S(1)} %max.11, pred[256,256]{0,1:T(8,128)(4,1)S(1)} %get-tuple-element.317, ...), kind=kOutput, calls=%fused_computation.8 | convolution fusion | flops 547356672 | bytes 17170432 | tf_op jit(solution)/shard_map/while/body/eval_jaxpr/cond/branch_1_fun/qkgs,skd->qkgd/dot_general | solution.py:79
  97.5 1.1 fusion.99
  98.6 10.8 %conditional.6 = ((f32[256,4,8]{0,2,1:T(8,128)S(1)}, f32[256,4,8]{0,2,1:T(8,128)S(1)}, f32[256,4,8,128]{3,0,2,1:T(8,128)})) conditional(s32[]{:T(128)} %convert_element_type.64, (f32[256,4,8]{0,2,1:T(8,128)S(1)}, f32[256,4,8]{0,2,1:T(8,128)S(1)}, f32[256,4,8,128]{3,0,2,1:T(8,128)}) %get-tuple-element.591, (pred[256,256]{0,1:T(8,128)(4,1)S(1)}, ...), branch_computations={%region_16.17_spmd, %region_17.20_spmd} | conditional | flops 1098924032 | bytes 36896800 | solution.py:87
  98.8 2.4 %fusion.19 = (f32[256,4,8]{0,2,1:T(8,128)S(1)}, f32[4,256,256,8]{2,1,3,0:T(8,128)S(1)}) fusion(pred[256,256]{0,1:T(8,128)(4,1)S(1)} %get-tuple-element.324, bf16[256,4,8,128]{3,2,1,0:T(8,128)(2,1)S(1)} %get-tuple-element.480, bf16[256,4,128]{0,2,1:T(8,128)(2,1)S(1)} %get-tuple-element.479), kind=kOutput, calls=%fused_computation.23 | convolution fusion | flops 543154176 | bytes 10846208 | tf_op jit(solution)/shard_map/while/body/eval_jaxpr/cond/branch_1_fun/qkgd,skd->qkgs/dot_general | solution.py:64
  101.2 1.8 %fusion.23 = f32[256,4,8]{0,2,1:T(8,128)S(1)} fusion(f32[4,256,256,8]{2,1,3,0:T(8,128)S(1)} %get-tuple-element.530, f32[256,4,8]{0,2,1:T(8,128)S(1)} %max.12, pred[256,256]{0,1:T(8,128)(4,1)S(1)} %get-tuple-element.324), kind=kLoop, calls=%fused_computation.27 | loop fusion | flops 8380416 | bytes 8519680 | tf_op jit(solution)/shard_map/while/body/eval_jaxpr/cond/branch_1_fun/reduce_sum | solution.py:78
  103.0 6.4 %bitcast_add_fusion.1 = f32[256,4,8,128]{3,0,2,1:T(8,128)} fusion(f32[256,4,8,128]{3,0,2,1:T(8,128)} %get-tuple-element.340, f32[256,4,8]{0,2,1:T(8,128)S(1)} %get-tuple-element.512, f32[4,256,256,8]{2,1,3,0:T(8,128)S(1)} %get-tuple-element.530, f32[256,4,8]{0,2,1:T(8,128)S(1)} %max.12, pred[256,256]{0,1:T(8,128)(4,1)S(1)} %get-tuple-element.324, ...), kind=kOutput, calls=%fused_computation.29 | convolution fusion | flops 547356672 | bytes 17170432 | tf_op jit(solution)/shard_map/while/body/eval_jaxpr/cond/branch_1_fun/qkgs,skd->qkgd/dot_general | solution.py:79
  109.4 1.1 fusion.98
  110.5 10.6 %conditional.7 = ((f32[256,4,8]{0,2,1:T(8,128)S(1)}, f32[256,4,8]{0,2,1:T(8,128)S(1)}, f32[256,4,8,128]{3,0,2,1:T(8,128)})) conditional(s32[]{:T(128)} %convert_element_type.62, (f32[256,4,8]{0,2,1:T(8,128)S(1)}, f32[256,4,8]{0,2,1:T(8,128)S(1)}, f32[256,4,8,128]{3,0,2,1:T(8,128)}) %get-tuple-element.592, (pred[256,256]{0,1:T(8,128)(4,1)S(1)}, ...), branch_computations={%region_20.21_spmd, %region_21.0_spmd} | conditional | flops 1098924032 | bytes 36896800 | solution.py:87
  110.5 2.4 %fusion.38 = (f32[256,4,8]{0,2,1:T(8,128)S(1)}, f32[4,256,256,8]{2,1,3,0:T(8,128)S(1)}) fusion(pred[256,256]{0,1:T(8,128)(4,1)S(1)} %get-tuple-element.345, bf16[256,4,8,128]{3,2,1,0:T(8,128)(2,1)S(1)} %get-tuple-element.487, bf16[256,4,128]{0,2,1:T(8,128)(2,1)S(1)} %get-tuple-element.486), kind=kOutput, calls=%fused_computation.44 | convolution fusion | flops 543154176 | bytes 10846208 | tf_op jit(solution)/shard_map/while/body/eval_jaxpr/cond/branch_1_fun/qkgd,skd->qkgs/dot_general | solution.py:64
  112.9 1.8 %fusion.42 = f32[256,4,8]{0,2,1:T(8,128)S(1)} fusion(f32[4,256,256,8]{2,1,3,0:T(8,128)S(1)} %get-tuple-element.532, f32[256,4,8]{0,2,1:T(8,128)S(1)} %max.13, pred[256,256]{0,1:T(8,128)(4,1)S(1)} %get-tuple-element.345), kind=kLoop, calls=%fused_computation.48 | loop fusion | flops 8380416 | bytes 8519680 | tf_op jit(solution)/shard_map/while/body/eval_jaxpr/cond/branch_1_fun/reduce_sum | solution.py:78
  114.8 6.4 %bitcast_add_fusion.2 = f32[256,4,8,128]{3,0,2,1:T(8,128)} fusion(f32[256,4,8,128]{3,0,2,1:T(8,128)} %get-tuple-element.349, f32[256,4,8]{0,2,1:T(8,128)S(1)} %get-tuple-element.514, f32[4,256,256,8]{2,1,3,0:T(8,128)S(1)} %get-tuple-element.532, f32[256,4,8]{0,2,1:T(8,128)S(1)} %max.13, pred[256,256]{0,1:T(8,128)(4,1)S(1)} %get-tuple-element.345, ...), kind=kOutput, calls=%fused_computation.50 | convolution fusion | flops 547356672 | bytes 17170432 | tf_op jit(solution)/shard_map/while/body/eval_jaxpr/cond/branch_1_fun/qkgs,skd->qkgd/dot_general | solution.py:79
  121.1 11.7 %conditional.8 = ((f32[256,4,8]{0,2,1:T(8,128)S(1)}, f32[256,4,8]{0,2,1:T(8,128)S(1)}, f32[256,4,8,128]{3,0,2,1:T(8,128)})) conditional(s32[]{:T(128)} %convert_element_type.60, (f32[256,4,8]{0,2,1:T(8,128)S(1)}, f32[256,4,8]{0,2,1:T(8,128)S(1)}, f32[256,4,8,128]{3,0,2,1:T(8,128)}) %get-tuple-element.593, (pred[256,256]{0,1:T(8,128)(4,1)S(1)}, ...), branch_computations={%region_24.25_spmd, %region_25.28_spmd} | conditional | flops 1098924032 | bytes 37945376 | solution.py:87
  121.1 1.1 fusion.96
  122.2 2.3 %fusion.57 = (f32[256,4,8]{0,2,1:T(8,128)S(1)}, f32[4,256,256,8]{2,1,3,0:T(8,128)S(1)}) fusion(pred[256,256]{0,1:T(8,128)(4,1)S(1)} %get-tuple-element.352, bf16[256,4,128,1]{0,2,3,1:T(8,128)(2,1)S(1)} %bitcast.198, bf16[256,4,8,128]{3,2,1,0:T(8,128)(2,1)S(1)} %get-tuple-element.494), kind=kOutput, calls=%fused_computation.65 | convolution fusion | flops 543154176 | bytes 10846208 | tf_op jit(solution)/shard_map/while/body/eval_jaxpr/cond/branch_1_fun/qkgd,skd->qkgs/dot_general | solution.py:64
  124.6 1.8 %fusion.61 = f32[256,4,8]{0,2,1:T(8,128)S(1)} fusion(f32[4,256,256,8]{2,1,3,0:T(8,128)S(1)} %get-tuple-element.536, f32[256,4,8]{0,2,1:T(8,128)S(1)} %max.14, pred[256,256]{0,1:T(8,128)(4,1)S(1)} %get-tuple-element.352), kind=kLoop, calls=%fused_computation.69 | loop fusion | flops 8380416 | bytes 8519680 | tf_op jit(solution)/shard_map/while/body/eval_jaxpr/cond/branch_1_fun/reduce_sum | solution.py:78
  126.4 6.4 %bitcast_add_fusion.3 = f32[256,4,8,128]{3,0,2,1:T(8,128)} fusion(f32[256,4,8,128]{3,0,2,1:T(8,128)} %get-tuple-element.356, f32[256,4,8]{0,2,1:T(8,128)S(1)} %get-tuple-element.516, bf16[256,4,128,1]{0,2,3,1:T(8,128)(2,1)S(1)} %bitcast.194, f32[4,256,256,8]{2,1,3,0:T(8,128)S(1)} %get-tuple-element.536, f32[256,4,8]{0,2,1:T(8,128)S(1)} %max.14, ...), kind=kOutput, calls=%fused_computation.71 | convolution fusion | flops 547356672 | bytes 17170432 | tf_op jit(solution)/shard_map/while/body/eval_jaxpr/cond/branch_1_fun/qkgs,skd->qkgd/dot_general | solution.py:79
  132.8 0.0 collective-permute-done.3
  132.8 11.6 %conditional.9 = ((f32[256,4,8]{0,2,1:T(8,128)S(1)}, f32[256,4,8,128]{3,0,2,1:T(8,128)})) conditional(s32[]{:T(128)} %convert_element_type.58, (f32[256,4,8]{0,2,1:T(8,128)S(1)}, f32[256,4,8,128]{3,0,2,1:T(8,128)}) %tuple.60, (pred[256,256]{0,1:T(8,128)(4,1)S(1)}, bf16[2,256,512]{1,2,0:T(8,128)(2,1)}, bf16[256,4,8,128]{3,2,1,0:T(8,128)(2,1)S(1)}, ...), branch_computations={%region_28.29_spmd, %region_29.0_spmd} | conditional | flops 1098924032 | bytes 37879832 | solution.py:87
  132.8 1.1 fusion.97
  133.9 2.3 %fusion.74 = (f32[256,4,8]{0,2,1:T(8,128)S(1)}, f32[4,256,256,8]{2,1,3,0:T(8,128)S(1)}) fusion(pred[256,256]{0,1:T(8,128)(4,1)S(1)} %get-tuple-element.359, bf16[256,4,128,1]{0,2,3,1:T(8,128)(2,1)S(1)} %bitcast.199, bf16[256,4,8,128]{3,2,1,0:T(8,128)(2,1)S(1)} %get-tuple-element.500), kind=kOutput, calls=%fused_computation.84 | convolution fusion | flops 543154176 | bytes 10846208 | tf_op jit(solution)/shard_map/while/body/eval_jaxpr/cond/branch_1_fun/qkgd,skd->qkgs/dot_general | solution.py:64
  136.2 1.8 %fusion.78 = f32[256,4,8]{0,2,1:T(8,128)S(1)} fusion(f32[4,256,256,8]{2,1,3,0:T(8,128)S(1)} %get-tuple-element.540, f32[256,4,8]{0,2,1:T(8,128)S(1)} %max.15, pred[256,256]{0,1:T(8,128)(4,1)S(1)} %get-tuple-element.359), kind=kLoop, calls=%fused_computation.88 | loop fusion | flops 8380416 | bytes 8519680 | tf_op jit(solution)/shard_map/while/body/eval_jaxpr/cond/branch_1_fun/reduce_sum | solution.py:78
  138.1 6.4 %bitcast_add_fusion.4 = f32[256,4,8,128]{3,0,2,1:T(8,128)} fusion(f32[256,4,8,128]{3,0,2,1:T(8,128)} %get-tuple-element.362, f32[256,4,8]{0,2,1:T(8,128)S(1)} %get-tuple-element.518, bf16[256,4,128,1]{0,2,3,1:T(8,128)(2,1)S(1)} %bitcast.195, f32[4,256,256,8]{2,1,3,0:T(8,128)S(1)} %get-tuple-element.540, f32[256,4,8]{0,2,1:T(8,128)S(1)} %max.15, ...), kind=kOutput, calls=%fused_computation.90 | convolution fusion | flops 547356672 | bytes 17170432 | tf_op jit(solution)/shard_map/while/body/eval_jaxpr/cond/branch_1_fun/qkgs,skd->qkgd/dot_general | solution.py:79
  144.4 2.9 %divide_convert_fusion = bf16[256,4,8,128]{3,0,2,1:T(8,128)(2,1)S(1)} fusion(f32[256,4,8,128]{3,0,2,1:T(8,128)} %get-tuple-element.389, f32[256,4,8]{0,2,1:T(8,128)S(1)} %get-tuple-element.390), kind=kLoop, calls=%fused_computation.101 | loop fusion | flops 2097152 | bytes 6324224 | tf_op jit(solution)/shard_map/convert_element_type | solution.py:99
  147.3 1.4 copy.95
  148.7 2.3 %all_to_all.59 = bf16[2,128,4096]{2,1,0:T(8,128)(2,1)} reshape(bf16[256,4,8,128]{3,2,1,0:T(8,128)(2,1)S(1)} %copy.95) | data formatting | bytes 4194304 | tf_op jit(solution)/shard_map/all_to_all | solution.py:102
  151.0 6.6 %all_to_all.67 = bf16[2,128,4096]{2,1,0:T(8,128)(2,1)S(1)} all-to-all(bf16[2,128,4096]{2,1,0:T(8,128)(2,1)} %all_to_all.59), channel_id=1, replica_groups=mesh['ctx'=256,'head'=2] {'head'}, dimensions={0} | all-to-all | bytes 4194304 | tf_op jit(solution)/shard_map/all_to_all | solution.py:102
  157.6 2.5 %copy.96 = bf16[128,2,4096]{0,2,1:T(8,128)(2,1)} copy(bf16[128,2,4096]{2,0,1:T(8,128)(2,1)S(1)} %bitcast.183) | data formatting | bytes 4194304 | tf_op jit(solution)/shard_map/all_to_all | solution.py:102
  160.0 4.1 %copy.97 = bf16[128,8192]{1,0:T(8,128)(2,1)} copy(bf16[128,8192]{0,1:T(8,128)(2,1)} %bitcast.184) | data formatting | bytes 4194304 | tf_op jit(solution)/shard_map/all_to_all | solution.py:102
  (28 shorter events, 0.2 us)
Async XLA Ops:
  0.0 23.1 %copy-start.3 = (s32[192]{0:T(256)S(1)}, s32[192]{0:T(256)}, u32[]{:S(2)}) copy-start(s32[192]{0:T(256)} %param.17) | copy-start | bytes 2308
  1.7 5.1 %all-to-all-start.2 = ((bf16[128,2,512]{2,0,1:T(8,128)(2,1)}), bf16[128,2,512]{2,0,1:T(8,128)(2,1)S(1)}, u32[]{:S(2)}, u32[]{:S(2)}) async-start(bf16[128,2,512]{2,0,1:T(8,128)(2,1)} %bitcast.173), calls=%async_computation.2 | async-start | bytes 524288 | tf_op jit(solution)/shard_map/all_to_all | solution.py:30
  6.8 5.0 %all-to-all-start = ((bf16[128,2,512]{2,0,1:T(8,128)(2,1)}), bf16[128,2,512]{2,0,1:T(8,128)(2,1)S(1)}, u32[]{:S(2)}, u32[]{:S(2)}) async-start(bf16[128,2,512]{2,0,1:T(8,128)(2,1)} %bitcast.174), calls=%async_computation | async-start | bytes 524288 | tf_op jit(solution)/shard_map/all_to_all | solution.py:29
  12.8 21.5 %collective-permute-start = (bf16[2,256,512]{1,2,0:T(8,128)(2,1)}, bf16[2,256,512]{1,2,0:T(8,128)(2,1)S(1)}, u32[]{:S(2)}, u32[]{:S(2)}) collective-permute-start(bf16[2,256,512]{1,2,0:T(8,128)(2,1)} %pad_maximum_fusion), channel_id=1, source_target_pairs={{0,2},{2,4},{4,6},{6,8},{8,10},{10,12},{12,14},{14,16},{16,18},{18... | collective-permute-start | bytes 1572872 | tf_op jit(solution)/shard_map/ppermute | solution.py:15
  19.3 61.7 %all-to-all-start.1 = ((bf16[128,2,4096]{2,0,1:T(8,128)(2,1)}), bf16[128,2,4096]{2,0,1:T(8,128)(2,1)S(1)}, u32[]{:S(2)}, u32[]{:S(2)}) async-start(bf16[128,2,4096]{2,0,1:T(8,128)(2,1)} %bitcast.182), calls=%async_computation.1 | async-start | bytes 4194304 | tf_op jit(solution)/shard_map/all_to_all | solution.py:28
  34.3 42.0 %copy-start.1 = (bf16[2,256,512]{1,2,0:T(8,128)(2,1)}, bf16[2,256,512]{1,2,0:T(8,128)(2,1)S(1)}, u32[]{:S(2)}) copy-start(bf16[2,256,512]{1,2,0:T(8,128)(2,1)S(1)} %collective-permute-done) | copy-start | bytes 1572868
  34.3 20.4 %collective-permute-start.1 = (bf16[2,256,512]{1,2,0:T(8,128)(2,1)S(1)}, bf16[2,256,512]{1,2,0:T(8,128)(2,1)S(1)}, u32[]{:S(2)}, u32[]{:S(2)}) collective-permute-start(bf16[2,256,512]{1,2,0:T(8,128)(2,1)S(1)} %collective-permute-done), channel_id=1, source_target_pairs={{0,2},{2,4},{4,6},{6,8},{8,10},{10,12},{12,14},{14,16},{16,18},{18... | collective-permute-start | bytes 1572872 | tf_op jit(solution)/shard_map/ppermute | solution.py:15
  54.7 21.6 %copy-start.2 = (bf16[2,256,512]{1,2,0:T(8,128)(2,1)}, bf16[2,256,512]{1,2,0:T(8,128)(2,1)S(1)}, u32[]{:S(2)}) copy-start(bf16[2,256,512]{1,2,0:T(8,128)(2,1)S(1)} %collective-permute-done.1) | copy-start | bytes 1572868
  54.7 19.7 %collective-permute-start.2 = (bf16[2,256,512]{1,2,0:T(8,128)(2,1)S(1)}, bf16[2,256,512]{1,2,0:T(8,128)(2,1)}, u32[]{:S(2)}, u32[]{:S(2)}) collective-permute-start(bf16[2,256,512]{1,2,0:T(8,128)(2,1)S(1)} %collective-permute-done.1), channel_id=1, source_target_pairs={{0,2},{2,4},{4,6},{6,8},{8,10},{10,12},{12,14},{14,16},{16,18},{18... | collective-permute-start | bytes 1572872 | tf_op jit(solution)/shard_map/ppermute | solution.py:15
  74.4 58.4 %collective-permute-start.3 = (bf16[2,256,512]{1,2,0:T(8,128)(2,1)}, bf16[2,256,512]{1,2,0:T(8,128)(2,1)}, u32[]{:S(2)}, u32[]{:S(2)}) collective-permute-start(bf16[2,256,512]{1,2,0:T(8,128)(2,1)} %collective-permute-done.2), channel_id=1, source_target_pairs={{0,2},{2,4},{4,6},{6,8},{8,10},{10,12},{12,14},{14,16},{16,18},{18... | collective-permute-start | bytes 1572872 | tf_op jit(solution)/shard_map/ppermute | solution.py:15
  81.0 1.3 copy-start
where the time goes:
time: 166 us; the launch traced here: 164 us
  waiting for transfers between devices  48 us (29%)
  matrix products  43.7 us (26%)
  local copies, waits for them, and re-layouts  27.3 us (16%)
  starting transfers between devices  19.8 us (12%)
  other arithmetic  15 us (9%)
  blocking collectives  6.61 us (4%)
  between operations  3.37 us (2%)
    ppermute x4, waiting for transfers between devices, from_behind(): return lax.ppermute(block, axis, route)  46.6 us
    dot_general x5, matrix products, update_tile(): jnp.einsum('qkgs,skd->qkgd', weights.astype(jnp.bfloat16), value_rows, pr...  31.9 us
    dot_general x5, matrix products, update_tile(): jnp.einsum('qkgd,skd->qkgs', query_blocked, key_rows, preferred_element_t...  11.7 us
    ppermute x4, starting transfers between devices, from_behind(): return lax.ppermute(block, axis, route)  9.12 us
    reduce_sum x5, other arithmetic, update_tile(): sum_new = row_sum * rescale + jnp.sum(weights, axis=-1)  9.07 us
    all_to_all x3, local copies, waits for them, and re-layouts, per_device(): lax.all_to_all(finished, 'head', split_axis=0, concat_axis=1, tiled=True)  8.82 us
    all_to_all x1, blocking collectives, per_device(): lax.all_to_all(finished, 'head', split_axis=0, concat_axis=1, tiled=True)  6.61 us
    slice x4, local copies, waits for them, and re-layouts, absorb(): value_rows = kv_pair[1].reshape(span_rows, kv_heads, HD)  4.25 us
  transfers between devices with their start and end apart: 7, of which 4 were waited for; matrix products, arithmetic and copies ran while one was open for 35% of the time, Pallas kernels for 0%

commit v1 on v0

v1 whole, which is shorter than its diff:
```python
import math

import jax
import jax.numpy as jnp
from jax import lax
from jax.experimental import pallas as pl
from jax.experimental.pallas import tpu as pltpu
from jax.sharding import PartitionSpec as P

H = 64
KVH = 8
HD = 128
GROUP = H // KVH
ROW = 4
BACK = 4
BLOCKS = 2 * (BACK + 1)
WINDOW = 2 * BACK + 1
T = 128
PAIR = 2
BIG = float(2**24)
MESH = pl.DeviceIdType.MESH


def kernel(
    lens_ref, q_hbm, k_hbm, v_hbm, out_ref,
    q_ref, buf, fk_ref, fq_ref, bias_ref, q_sem, kv_sem, ssem, rsem,
):
    c = lax.axis_index("ctx")
    i = lax.axis_index("head")
    n = lax.axis_size("ctx")
    x = c % ROW
    first = (c // ROW) * ROW
    right = (first + (x + 1) % ROW, i)
    left = (first + (x + ROW - 1) % ROW, i)
    up = ((c + ROW) % n, i)
    down = ((c + n - ROW) % n, i)
    partner = (c, 1 - i)
    middle = ((x + 1) // 2) % 2 == 1

    def block(slot):
        return 2 * (BACK - slot) + i

    def own_k(h):
        return pltpu.make_async_copy(
            k_hbm.at[:, pl.ds(pl.multiple_of(h * HD, HD), HD)], buf.at[h, block(0), 0], kv_sem.at[h, 0]
        )

    def own_v(h):
        return pltpu.make_async_copy(
            v_hbm.at[:, pl.ds(pl.multiple_of(h * HD, HD), HD)], buf.at[h, block(0), 1], kv_sem.at[h, 1]
        )

    q_copy = pltpu.make_async_copy(q_hbm, q_ref, q_sem)

    def send(h, src, dst, s, r, device):
        return pltpu.make_async_remote_copy(
            src_ref=buf.at[h, src],
            dst_ref=buf.at[h, dst],
            send_sem=ssem.at[h, s],
            recv_sem=rsem.at[h, r],
            device_id=device,
            device_id_type=MESH,
        )

    def to_up(h):
        return send(h, block(0), block(BACK), 0, BACK, up)

    def to_right(h):
        return send(h, i + 8 * (1 - (x + 1) // ROW), block(1), 1, 1, right)

    def to_left(h):
        return send(h, i + 8 * ((ROW - 1 - x) // (ROW - 1)), block(3), 3, 3, left)

    def relay_right(h):
        return send(h, block(1), block(2), 2, 2, right)

    def relay_left(h):
        return send(h, block(3), block(2), 9, 2, left)

    def share(h, slot):
        return send(h, block(slot), block(slot), 4 + slot, 5 + slot, partner)

    def arrived(h, slot):
        send(h, block(slot), block(slot), 0, slot, partner).wait_recv()

    def shared(h, slot):
        other = 2 * (BACK - slot) + 1 - i
        send(h, other, other, 0, 5 + slot, partner).wait_recv()

    def stage1(h):
        arrived(h, 4)
        to_left(h).start()
        to_right(h).start()
        share(h, 4).start()

    def stage2(h):
        arrived(h, 1)
        arrived(h, 3)

        @pl.when(middle)
        def _():
            relay_left(h).start()
            relay_right(h).start()

        share(h, 1).start()
        share(h, 3).start()

    def stage3(h):
        arrived(h, 2)
        share(h, 2).start()

    for h in range(KVH):
        own_k(h).start()
        own_v(h).start()
    barrier = pltpu.get_barrier_semaphore()
    for device in (up, down, left, right, partner):
        pl.semaphore_signal(barrier, inc=1, device_id=device, device_id_type=MESH)
    pl.semaphore_wait(barrier, 5)
    for h in range(KVH):
        own_k(h).wait()
        own_v(h).wait()
        to_up(h).start()
    for h in range(KVH):
        share(h, 0).start()
    q_copy.start()

    docs = lens_ref.shape[1]
    lens = lens_ref[...].astype(jnp.float32)
    ia = lax.broadcasted_iota(jnp.int32, (docs, docs), 0)
    ib = lax.broadcasted_iota(jnp.int32, (docs, docs), 1)
    column = jnp.sum(jnp.where(ia == ib, lens, 0.0), axis=1, keepdims=True)
    ends = jnp.sum(jnp.where(ia <= ib, column, 0.0), axis=0, keepdims=True)
    begin = c * (2 * T) + i * T - (WINDOW - 1) * T
    position = begin + lax.broadcasted_iota(jnp.int32, (WINDOW * T, 1), 0)
    before = (ends <= position.astype(jnp.float32)).astype(jnp.float32)
    doc = jnp.sum(before, axis=1, keepdims=True)
    doc = doc - doc[(WINDOW - 1) * T:(WINDOW - 1) * T + 1, :]
    lane = lax.broadcasted_iota(jnp.int32, (WINDOW * T, T), 1).astype(jnp.float32)
    same = (doc == lane) & (position >= 0)
    fk_ref[...] = jnp.where(same, 0.0, 1.0).astype(jnp.bfloat16)
    fq_ref[...] = jnp.where(same[(WINDOW - 1) * T:], -BIG, 0.0).astype(jnp.bfloat16)
    row = lax.broadcasted_iota(jnp.int32, (PAIR * T, T), 0) % T
    col = lax.broadcasted_iota(jnp.int32, (PAIR * T, T), 1)
    bias_ref[...] = jnp.where(col <= row, 0.0, -BIG)

    def compute(h):
        keys = buf[h, pl.ds(i, WINDOW), 0].reshape(WINDOW * T, HD)
        values = buf[h, pl.ds(i, WINDOW), 1].reshape(WINDOW * T, HD)
        keys = jnp.concatenate([keys, fk_ref[...]], axis=1)
        values = jnp.concatenate([values, jnp.ones((WINDOW * T, HD), jnp.bfloat16)], axis=1)
        factor = jnp.float32(HD**-0.5 * math.log2(math.e))
        for pair in range(GROUP // PAIR):
            at = [pl.multiple_of((h * GROUP + pair * PAIR + g) * HD, HD) for g in range(PAIR)]
            q = jnp.concatenate(
                [jnp.concatenate([q_ref[:, pl.ds(a, HD)], fq_ref[...]], axis=1) for a in at], axis=0
            )
            s = lax.dot_general(q, keys, (((1,), (1,)), ((), ())), preferred_element_type=jnp.float32)
            far, near = s[:, :(WINDOW - 1) * T], s[:, (WINDOW - 1) * T:] + bias_ref[...]
            s = jnp.concatenate([far, near], axis=1)
            top = jnp.max(s, axis=1, keepdims=True)
            w = jnp.exp2((s - top) * factor).astype(jnp.bfloat16)
            o = jnp.dot(w, values, preferred_element_type=jnp.float32)
            o = (o[:, :HD] / o[:, HD:]).astype(jnp.bfloat16)
            for g in range(PAIR):
                out_ref[:, pl.ds(at[g], HD)] = o[g * T:(g + 1) * T]

    for h in range(3):
        stage1(h)
    stage2(0)
    stage1(3)
    stage2(1)
    stage3(0)
    q_copy.wait()

    @pl.loop(0, KVH)
    def _(h):
        @pl.when(h + 4 < KVH)
        def _():
            stage1(h + 4)

        @pl.when(h + 2 < KVH)
        def _():
            stage2(h + 2)

        @pl.when(h + 1 < KVH)
        def _():
            stage3(h + 1)

        for slot in range(BACK + 1):
            shared(h, slot)
        compute(h)

    @pl.loop(0, KVH)
    def _(h):
        to_up(h).wait_send()
        to_right(h).wait_send()
        to_left(h).wait_send()
        for slot in range(BACK + 1):
            share(h, slot).wait_send()

        @pl.when(middle)
        def _():
            relay_left(h).wait_send()
            relay_right(h).wait_send()


def per_device(queries, keys, values, doc_lengths):
    any_space = pl.BlockSpec(memory_space=pl.ANY)
    vmem = pl.BlockSpec(memory_space=pltpu.VMEM)
    return pl.pallas_call(
        kernel,
        out_shape=jax.ShapeDtypeStruct(queries.shape, queries.dtype),
        in_specs=[vmem, any_space, any_space, any_space],
        out_specs=vmem,
        scratch_shapes=[
            pltpu.VMEM((T, H * HD), jnp.bfloat16),
            pltpu.VMEM((KVH, BLOCKS, 2, T, HD), jnp.bfloat16),
            pltpu.VMEM((WINDOW * T, HD), jnp.bfloat16),
            pltpu.VMEM((T, HD), jnp.bfloat16),
            pltpu.VMEM((PAIR * T, T), jnp.float32),
            pltpu.SemaphoreType.DMA,
            pltpu.SemaphoreType.DMA((KVH, 2)),
            pltpu.SemaphoreType.DMA((KVH, 10)),
            pltpu.SemaphoreType.DMA((KVH, 10)),
        ],
        compiler_params=pltpu.CompilerParams(collective_id=0, has_side_effects=True),
    )(doc_lengths.reshape(1, -1), queries, keys, values)


def solution(mesh):
    placed = (P(("ctx", "head"), None), P(("ctx", "head"), None), P(("ctx", "head"), None), P())
    return jax.shard_map(
        per_device, mesh=mesh, in_specs=placed, out_specs=P(("ctx", "head"), None), check_vma=False
    )
```

time: 166 us -> 59.2 us (0.36)
  the two profiles are of different devices: /device:TPU:256 before, /device:TPU:1 now
where the time goes in v1:
time: 59.2 us; the launch traced here: 58.9 us
  Pallas kernels  55.8 us (94%)
  local copies, waits for them, and re-layouts  3.1 us (5%)
    pallas_call x1, Pallas kernels, per_device(): pl.pallas_call(kernel, out_shape=jax.ShapeDtypeStruct(queries.shape, quer...  55.8 us
    unnamed x1, local copies, waits for them, and re-layouts  3.1 us

profile of v1, /device:TPU:1, one launch (start us, length us, event | category | flops | bytes accessed | tf_op | source)
XLA Modules:
  0.0 58.9 jit_solution(8949859962562444923)
XLA Ops:
  0.0 55.8 %shard_map.46 = bf16[128,8192]{1,0:T(8,128)(2,1)} custom-call(s32[1,192]{1,0:T(1,128)} %bitcast.1, bf16[128,8192]{1,0:T(8,128)(2,1)} %q_hbm.1, bf16[128,1024]{1,0:T(8,128)(2,1)} %k_hbm.1, bf16[128,1024]{1,0:T(8,128)(2,1)} %v_hbm.1), custom_call_target="tpu_custom_call" | custom-call | tf_op jit(solution)/shard_map/pallas_call | solution.py:210
  55.9 3.1 %copy.6 = bf16[128,8192]{1,0:T(8,128)(2,1)} copy(bf16[128,8192]{1,0:T(8,128)(2,1)} %shard_map.46) | data formatting | bytes 4194304

commit v2 on v1

--- a/solution.py
+++ b/solution.py
@@ -22,8 +22,8 @@
 
 
 def kernel(
-    lens_ref, q_hbm, k_hbm, v_hbm, out_ref,
-    q_ref, buf, fk_ref, fq_ref, bias_ref, q_sem, kv_sem, ssem, rsem,
+    lens_hbm, q_hbm, k_hbm, v_hbm, out_ref,
+    lens_ref, q_ref, buf, fk_ref, fq_ref, bias_ref, lens_sem, q_sem, kv_sem, ssem, rsem,
 ):
     c = lax.axis_index("ctx")
     i = lax.axis_index("head")
@@ -35,22 +35,19 @@
     up = ((c + ROW) % n, i)
     down = ((c + n - ROW) % n, i)
     partner = (c, 1 - i)
-    middle = ((x + 1) // 2) % 2 == 1
+    across = (first + (x + 2) % ROW, i)
+    has_down = c >= ROW
+    has_up = c < n - ROW
 
     def block(slot):
         return 2 * (BACK - slot) + i
 
-    def own_k(h):
-        return pltpu.make_async_copy(
-            k_hbm.at[:, pl.ds(pl.multiple_of(h * HD, HD), HD)], buf.at[h, block(0), 0], kv_sem.at[h, 0]
-        )
-
-    def own_v(h):
-        return pltpu.make_async_copy(
-            v_hbm.at[:, pl.ds(pl.multiple_of(h * HD, HD), HD)], buf.at[h, block(0), 1], kv_sem.at[h, 1]
-        )
+    def own(h, which, slot=0):
+        source = (k_hbm, v_hbm)[which].at[:, pl.ds(pl.multiple_of(h * HD, HD), HD)]
+        return pltpu.make_async_copy(source, buf.at[h, block(slot), which], kv_sem.at[h, which + slot // 2])
 
     q_copy = pltpu.make_async_copy(q_hbm, q_ref, q_sem)
+    lens_copy = pltpu.make_async_copy(lens_hbm, lens_ref, lens_sem)
 
     def send(h, src, dst, s, r, device):
         return pltpu.make_async_remote_copy(
@@ -71,11 +68,8 @@
     def to_left(h):
         return send(h, i + 8 * ((ROW - 1 - x) // (ROW - 1)), block(3), 3, 3, left)
 
-    def relay_right(h):
-        return send(h, block(1), block(2), 2, 2, right)
-
-    def relay_left(h):
-        return send(h, block(3), block(2), 9, 2, left)
+    def to_across(h):
+        return send(h, i + 8 * (1 - x // 2), block(2), 2, 2, across)
 
     def share(h, slot):
         return send(h, block(slot), block(slot), 4 + slot, 5 + slot, partner)
@@ -88,42 +82,59 @@
         send(h, other, other, 0, 5 + slot, partner).wait_recv()
 
     def stage1(h):
-        arrived(h, 4)
+        @pl.when(has_down)
+        def _():
+            arrived(h, 4)
+
         to_left(h).start()
         to_right(h).start()
+        to_across(h).start()
         share(h, 4).start()
 
     def stage2(h):
-        arrived(h, 1)
-        arrived(h, 3)
-
-        @pl.when(middle)
-        def _():
-            relay_left(h).start()
-            relay_right(h).start()
-
-        share(h, 1).start()
-        share(h, 3).start()
-
-    def stage3(h):
-        arrived(h, 2)
-        share(h, 2).start()
+        for slot in (1, 3, 2):
+            arrived(h, slot)
+            share(h, slot).start()
 
     for h in range(KVH):
-        own_k(h).start()
-        own_v(h).start()
+        own(h, 0).start()
+        own(h, 1).start()
+    lens_copy.start()
     barrier = pltpu.get_barrier_semaphore()
-    for device in (up, down, left, right, partner):
+    for device in (left, right, across, partner):
         pl.semaphore_signal(barrier, inc=1, device_id=device, device_id_type=MESH)
-    pl.semaphore_wait(barrier, 5)
+
+    @pl.when(has_down)
+    def _():
+        pl.semaphore_signal(barrier, inc=1, device_id=down, device_id_type=MESH)
+
+    @pl.when(has_up)
+    def _():
+        pl.semaphore_signal(barrier, inc=1, device_id=up, device_id_type=MESH)
+
+    @pl.when(c < ROW)
+    def _():
+        for h in range(KVH):
+            own(h, 0, BACK).start()
+            own(h, 1, BACK).start()
+        for h in range(KVH):
+            own(h, 0, BACK).wait()
+            own(h, 1, BACK).wait()
+
+    pl.semaphore_wait(barrier, 4 + jnp.minimum(c // ROW, 1) + jnp.minimum((n - 1 - c) // ROW, 1))
     for h in range(KVH):
-        own_k(h).wait()
-        own_v(h).wait()
-        to_up(h).start()
+        own(h, 0).wait()
+        own(h, 1).wait()
+
+        @pl.when(has_up)
+        def _():
+            to_up(h).start()
+
     for h in range(KVH):
         share(h, 0).start()
     q_copy.start()
 
+    lens_copy.wait()
     docs = lens_ref.shape[1]
     lens = lens_ref[...].astype(jnp.float32)
     ia = lax.broadcasted_iota(jnp.int32, (docs, docs), 0)
@@ -164,12 +175,9 @@
             for g in range(PAIR):
                 out_ref[:, pl.ds(at[g], HD)] = o[g * T:(g + 1) * T]
 
-    for h in range(3):
+    for h in range(4):
         stage1(h)
     stage2(0)
-    stage1(3)
-    stage2(1)
-    stage3(0)
     q_copy.wait()
 
     @pl.loop(0, KVH)
@@ -178,13 +186,9 @@
         def _():
             stage1(h + 4)
 
-        @pl.when(h + 2 < KVH)
-        def _():
-            stage2(h + 2)
-
         @pl.when(h + 1 < KVH)
         def _():
-            stage3(h + 1)
+            stage2(h + 1)
 
         for slot in range(BACK + 1):
             shared(h, slot)
@@ -192,39 +196,42 @@
 
     @pl.loop(0, KVH)
     def _(h):
-        to_up(h).wait_send()
+        @pl.when(has_up)
+        def _():
+            to_up(h).wait_send()
+
         to_right(h).wait_send()
         to_left(h).wait_send()
+        to_across(h).wait_send()
         for slot in range(BACK + 1):
             share(h, slot).wait_send()
 
-        @pl.when(middle)
-        def _():
-            relay_left(h).wait_send()
-            relay_right(h).wait_send()
-
 
 def per_device(queries, keys, values, doc_lengths):
-    any_space = pl.BlockSpec(memory_space=pl.ANY)
+    hbm = pl.BlockSpec(memory_space=pltpu.HBM)
     vmem = pl.BlockSpec(memory_space=pltpu.VMEM)
+    lengths = doc_lengths.reshape(1, -1)
+    operands = [pltpu.with_memory_space_constraint(a, pltpu.HBM) for a in (lengths, queries, keys, values)]
     return pl.pallas_call(
         kernel,
         out_shape=jax.ShapeDtypeStruct(queries.shape, queries.dtype),
-        in_specs=[vmem, any_space, any_space, any_space],
+        in_specs=[hbm, hbm, hbm, hbm],
         out_specs=vmem,
         scratch_shapes=[
+            pltpu.VMEM((1, doc_lengths.shape[0]), jnp.int32),
             pltpu.VMEM((T, H * HD), jnp.bfloat16),
             pltpu.VMEM((KVH, BLOCKS, 2, T, HD), jnp.bfloat16),
             pltpu.VMEM((WINDOW * T, HD), jnp.bfloat16),
             pltpu.VMEM((T, HD), jnp.bfloat16),
             pltpu.VMEM((PAIR * T, T), jnp.float32),
             pltpu.SemaphoreType.DMA,
-            pltpu.SemaphoreType.DMA((KVH, 2)),
+            pltpu.SemaphoreType.DMA,
+            pltpu.SemaphoreType.DMA((KVH, 4)),
             pltpu.SemaphoreType.DMA((KVH, 10)),
             pltpu.SemaphoreType.DMA((KVH, 10)),
         ],
-        compiler_params=pltpu.CompilerParams(collective_id=0, has_side_effects=True),
-    )(doc_lengths.reshape(1, -1), queries, keys, values)
+        compiler_params=pltpu.CompilerParams(collective_id=0, has_side_effects=True, vmem_limit_bytes=24 << 20),
+    )(*operands)
 
 
 def solution(mesh):

time: 59.2 us -> 42.5 us (0.72)
  the two profiles are of different devices: /device:TPU:1 before, /device:TPU:256 now
where the time goes in v2:
time: 42.5 us; the launch traced here: 42.3 us
  Pallas kernels  41 us (96%)
  local copies, waits for them, and re-layouts  1.32 us (3%)
    pallas_call x1, Pallas kernels, per_device(): pl.pallas_call(kernel, out_shape=jax.ShapeDtypeStruct(queries.shape, quer...  41 us
    unnamed x1, local copies, waits for them, and re-layouts  1.32 us

profile of v2, /device:TPU:256, one launch (start us, length us, event | category | flops | bytes accessed | tf_op | source)
XLA Modules:
  0.0 42.3 jit_solution(10433742122234172409)
XLA Ops:
  0.0 41.0 %shard_map.46 = bf16[128,8192]{1,0:T(8,128)(2,1)S(1)} custom-call(s32[1,192]{1,0:T(1,128)} %bitcast.1, bf16[128,8192]{1,0:T(8,128)(2,1)} %q_hbm.1, bf16[128,1024]{1,0:T(8,128)(2,1)} %k_hbm.1, bf16[128,1024]{1,0:T(8,128)(2,1)} %v_hbm.1), custom_call_target="tpu_custom_call" | custom-call | tf_op jit(solution)/shard_map/pallas_call | solution.py:215
  41.0 1.3 %copy.6 = bf16[128,8192]{1,0:T(8,128)(2,1)} copy(bf16[128,8192]{1,0:T(8,128)(2,1)S(1)} %shard_map.46) | data formatting | bytes 4194304

commit v3 on v2

--- a/solution.py
+++ b/solution.py
@@ -17,13 +17,16 @@
 WINDOW = 2 * BACK + 1
 T = 128
 PAIR = 2
+UNITS = GROUP // PAIR
+STEPS = UNITS // 2
+EARLY = 3
 BIG = float(2**24)
 MESH = pl.DeviceIdType.MESH
 
 
 def kernel(
     lens_hbm, q_hbm, k_hbm, v_hbm, out_ref,
-    lens_ref, q_ref, buf, fk_ref, fq_ref, bias_ref, lens_sem, q_sem, kv_sem, ssem, rsem,
+    lens_ref, q_ref, buf, fk_ref, fq_ref, bias_ref, s_a, s_b, w_a, w_b, lens_sem, q_sem, kv_sem, ssem, rsem,
 ):
     c = lax.axis_index("ctx")
     i = lax.axis_index("head")
@@ -49,10 +52,10 @@
     q_copy = pltpu.make_async_copy(q_hbm, q_ref, q_sem)
     lens_copy = pltpu.make_async_copy(lens_hbm, lens_ref, lens_sem)
 
-    def send(h, src, dst, s, r, device):
+    def send(h, src, dst, s, r, device, which=None):
         return pltpu.make_async_remote_copy(
-            src_ref=buf.at[h, src],
-            dst_ref=buf.at[h, dst],
+            src_ref=buf.at[h, src] if which is None else buf.at[h, src, which],
+            dst_ref=buf.at[h, dst] if which is None else buf.at[h, dst, which],
             send_sem=ssem.at[h, s],
             recv_sem=rsem.at[h, r],
             device_id=device,
@@ -68,8 +71,19 @@
     def to_left(h):
         return send(h, i + 8 * ((ROW - 1 - x) // (ROW - 1)), block(3), 3, 3, left)
 
+    sends_across = (x == 1) | (x == 2)
+    relays_right = x < ROW - 1
+    relays_left = x > 0
+    passes = 1 - x // 2
+
     def to_across(h):
-        return send(h, i + 8 * (1 - x // 2), block(2), 2, 2, across)
+        return send(h, i + 8 * (1 - x // 2), block(2), 2, 2, across, 0)
+
+    def relay_right(h):
+        return send(h, block(1), block(2), 9, 10, right, 1)
+
+    def relay_left(h):
+        return send(h, block(3), block(2), 10, 2 + 8 * passes, left, passes)
 
     def share(h, slot):
         return send(h, block(slot), block(slot), 4 + slot, 5 + slot, partner)
@@ -81,20 +95,47 @@
         other = 2 * (BACK - slot) + 1 - i
         send(h, other, other, 0, 5 + slot, partner).wait_recv()
 
-    def stage1(h):
+    def stage1(h, ahead):
         @pl.when(has_down)
         def _():
             arrived(h, 4)
 
         to_left(h).start()
-        to_right(h).start()
-        to_across(h).start()
+
+        @pl.when(x == ROW - 1)
+        def _():
+            to_right(h).start()
+
+        @pl.when(x == 2)
+        def _():
+            to_across(h).start()
+
         share(h, 4).start()
 
+        @pl.when((x < ROW - 1) & ahead)
+        def _():
+            to_right(jnp.minimum(h + EARLY, KVH - 1)).start()
+
     def stage2(h):
-        for slot in (1, 3, 2):
-            arrived(h, slot)
-            share(h, slot).start()
+        arrived(h, 1)
+
+        @pl.when(relays_right)
+        def _():
+            relay_right(h).start()
+
+        arrived(h, 3)
+
+        @pl.when(relays_left)
+        def _():
+            relay_left(h).start()
+
+        share(h, 1).start()
+        share(h, 3).start()
+
+    def stage3(h):
+        send(h, block(2), block(2), 0, 2, partner, 0).wait_recv()
+        send(h, block(2), block(2), 0, 10, partner, 1).wait_recv()
+        share(h, 2).start()
 
     for h in range(KVH):
         own(h, 0).start()
@@ -129,6 +170,16 @@
         @pl.when(has_up)
         def _():
             to_up(h).start()
+
+    @pl.when(x < ROW - 1)
+    def _():
+        for h in range(EARLY):
+            to_right(h).start()
+
+    @pl.when(x == 1)
+    def _():
+        for h in range(KVH):
+            to_across(h).start()
 
     for h in range(KVH):
         share(h, 0).start()
@@ -154,45 +205,78 @@
     col = lax.broadcasted_iota(jnp.int32, (PAIR * T, T), 1)
     bias_ref[...] = jnp.where(col <= row, 0.0, -BIG)
 
-    def compute(h):
-        keys = buf[h, pl.ds(i, WINDOW), 0].reshape(WINDOW * T, HD)
-        values = buf[h, pl.ds(i, WINDOW), 1].reshape(WINDOW * T, HD)
-        keys = jnp.concatenate([keys, fk_ref[...]], axis=1)
-        values = jnp.concatenate([values, jnp.ones((WINDOW * T, HD), jnp.bfloat16)], axis=1)
-        factor = jnp.float32(HD**-0.5 * math.log2(math.e))
-        for pair in range(GROUP // PAIR):
-            at = [pl.multiple_of((h * GROUP + pair * PAIR + g) * HD, HD) for g in range(PAIR)]
-            q = jnp.concatenate(
-                [jnp.concatenate([q_ref[:, pl.ds(a, HD)], fq_ref[...]], axis=1) for a in at], axis=0
-            )
-            s = lax.dot_general(q, keys, (((1,), (1,)), ((), ())), preferred_element_type=jnp.float32)
-            far, near = s[:, :(WINDOW - 1) * T], s[:, (WINDOW - 1) * T:] + bias_ref[...]
-            s = jnp.concatenate([far, near], axis=1)
-            top = jnp.max(s, axis=1, keepdims=True)
-            w = jnp.exp2((s - top) * factor).astype(jnp.bfloat16)
-            o = jnp.dot(w, values, preferred_element_type=jnp.float32)
-            o = (o[:, :HD] / o[:, HD:]).astype(jnp.bfloat16)
-            for g in range(PAIR):
-                out_ref[:, pl.ds(at[g], HD)] = o[g * T:(g + 1) * T]
+    def heads_of(unit):
+        return [pl.multiple_of((unit * PAIR + g) * HD, HD) for g in range(PAIR)]
+
+    def window(unit, which):
+        return buf[unit // UNITS, pl.ds(i, WINDOW), which].reshape(WINDOW * T, HD)
+
+    def score(unit, s_ref):
+        keys = jnp.concatenate([window(unit, 0), fk_ref[...]], axis=1)
+        q = jnp.concatenate(
+            [jnp.concatenate([q_ref[:, pl.ds(a, HD)], fq_ref[...]], axis=1) for a in heads_of(unit)], axis=0
+        )
+        s_ref[...] = lax.dot_general(q, keys, (((1,), (1,)), ((), ())), preferred_element_type=jnp.float32)
+
+    def weigh(s_ref, w_ref):
+        far, near = s_ref[:, :(WINDOW - 1) * T], s_ref[:, (WINDOW - 1) * T:] + bias_ref[...]
+        s = jnp.concatenate([far, near], axis=1)
+        top = jnp.max(s, axis=1, keepdims=True)
+        w_ref[...] = jnp.exp2((s - top) * jnp.float32(HD**-0.5 * math.log2(math.e))).astype(jnp.bfloat16)
+
+    def attend(unit, w_ref):
+        values = jnp.concatenate([window(unit, 1), jnp.ones((WINDOW * T, HD), jnp.bfloat16)], axis=1)
+        o = jnp.dot(w_ref[...], values, preferred_element_type=jnp.float32)
+        o = (o[:, :HD] / o[:, HD:]).astype(jnp.bfloat16)
+        for g, a in enumerate(heads_of(unit)):
+            out_ref[:, pl.ds(a, HD)] = o[g * T:(g + 1) * T]
+
+    last = KVH * UNITS - 1
+
+    def clamped(unit):
+        return jnp.maximum(unit, 0)
+
+    def two_units(j):
+        attend(clamped(2 * j - 2), w_a)
+        weigh(s_b, w_b)
+        score(2 * j, s_a)
+        attend(clamped(2 * j - 1), w_b)
+        weigh(s_a, w_a)
+        score(2 * j + 1, s_b)
 
     for h in range(4):
-        stage1(h)
+        stage1(h, h + EARLY < KVH)
     stage2(0)
+    stage2(1)
+    stage3(0)
     q_copy.wait()
 
-    @pl.loop(0, KVH)
-    def _(h):
-        @pl.when(h + 4 < KVH)
-        def _():
-            stage1(h + 4)
-
-        @pl.when(h + 1 < KVH)
-        def _():
-            stage2(h + 1)
-
-        for slot in range(BACK + 1):
-            shared(h, slot)
-        compute(h)
+    @pl.loop(0, KVH * STEPS)
+    def _(j):
+        h = j // STEPS
+
+        @pl.when(j % STEPS == 0)
+        def _():
+            @pl.when(h + 4 < KVH)
+            def _():
+                stage1(h + 4, h + 4 + EARLY < KVH)
+
+            for slot in range(BACK + 1):
+                shared(h, slot)
+
+        @pl.when((j % STEPS == 0) & (h + 2 < KVH))
+        def _():
+            stage2(h + 2)
+
+        @pl.when((j % STEPS == STEPS - 1) & (h + 1 < KVH))
+        def _():
+            stage3(h + 1)
+
+        two_units(j)
+
+    attend(last - 1, w_a)
+    weigh(s_b, w_b)
+    attend(last, w_b)
 
     @pl.loop(0, KVH)
     def _(h):
@@ -202,9 +286,20 @@
 
         to_right(h).wait_send()
         to_left(h).wait_send()
-        to_across(h).wait_send()
         for slot in range(BACK + 1):
             share(h, slot).wait_send()
+
+        @pl.when(sends_across)
+        def _():
+            to_across(h).wait_send()
+
+        @pl.when(relays_right)
+        def _():
+            relay_right(h).wait_send()
+
+        @pl.when(relays_left)
+        def _():
+            relay_left(h).wait_send()
 
 
 def per_device(queries, keys, values, doc_lengths):
@@ -224,11 +319,15 @@
             pltpu.VMEM((WINDOW * T, HD), jnp.bfloat16),
             pltpu.VMEM((T, HD), jnp.bfloat16),
             pltpu.VMEM((PAIR * T, T), jnp.float32),
+            pltpu.VMEM((PAIR * T, WINDOW * T), jnp.float32),
+            pltpu.VMEM((PAIR * T, WINDOW * T), jnp.float32),
+            pltpu.VMEM((PAIR * T, WINDOW * T), jnp.bfloat16),
+            pltpu.VMEM((PAIR * T, WINDOW * T), jnp.bfloat16),
             pltpu.SemaphoreType.DMA,
             pltpu.SemaphoreType.DMA,
             pltpu.SemaphoreType.DMA((KVH, 4)),
-            pltpu.SemaphoreType.DMA((KVH, 10)),
-            pltpu.SemaphoreType.DMA((KVH, 10)),
+            pltpu.SemaphoreType.DMA((KVH, 11)),
+            pltpu.SemaphoreType.DMA((KVH, 11)),
         ],
         compiler_params=pltpu.CompilerParams(collective_id=0, has_side_effects=True, vmem_limit_bytes=24 << 20),
     )(*operands)

time: 42.5 us -> 43.9 us (1.033)
  the two profiles are of different devices: /device:TPU:256 before, /device:TPU:321 now
where the time goes in v3:
time: 43.9 us; the launch traced here: 43.7 us
  Pallas kernels  42.4 us (97%)
  local copies, waits for them, and re-layouts  1.32 us (3%)
    pallas_call x1, Pallas kernels, per_device(): pl.pallas_call(kernel, out_shape=jax.ShapeDtypeStruct(queries.shape, quer...  42.4 us
    unnamed x1, local copies, waits for them, and re-layouts  1.32 us

profile of v3, /device:TPU:321, one launch (start us, length us, event | category | flops | bytes accessed | tf_op | source)
XLA Modules:
  0.0 43.7 jit_solution(6497184351956359726)
XLA Ops:
  0.0 42.4 %shard_map.46 = bf16[128,8192]{1,0:T(8,128)(2,1)S(1)} custom-call(s32[1,192]{1,0:T(1,128)} %bitcast.1, bf16[128,8192]{1,0:T(8,128)(2,1)} %q_hbm.1, bf16[128,1024]{1,0:T(8,128)(2,1)} %k_hbm.1, bf16[128,1024]{1,0:T(8,128)(2,1)} %v_hbm.1), custom_call_target="tpu_custom_call" | custom-call | tf_op jit(solution)/shard_map/pallas_call | solution.py:310
  42.4 1.3 %copy.6 = bf16[128,8192]{1,0:T(8,128)(2,1)} copy(bf16[128,8192]{1,0:T(8,128)(2,1)S(1)} %shard_map.46) | data formatting | bytes 4194304

commit v4 on v2

--- a/solution.py
+++ b/solution.py
@@ -23,7 +23,7 @@
 
 def kernel(
     lens_hbm, q_hbm, k_hbm, v_hbm, out_ref,
-    lens_ref, q_ref, buf, fk_ref, fq_ref, bias_ref, lens_sem, q_sem, kv_sem, ssem, rsem,
+    lens_ref, q_ref, buf, fk_ref, fq_ref, bias_ref, lens_sem, q_sem, fill_sem, kv_sem, ssem, rsem,
 ):
     c = lax.axis_index("ctx")
     i = lax.axis_index("head")
@@ -44,7 +44,7 @@
 
     def own(h, which, slot=0):
         source = (k_hbm, v_hbm)[which].at[:, pl.ds(pl.multiple_of(h * HD, HD), HD)]
-        return pltpu.make_async_copy(source, buf.at[h, block(slot), which], kv_sem.at[h, which + slot // 2])
+        return pltpu.make_async_copy(source, buf.at[h, block(slot), which], fill_sem if slot else kv_sem.at[h])
 
     q_copy = pltpu.make_async_copy(q_hbm, q_ref, q_sem)
     lens_copy = pltpu.make_async_copy(lens_hbm, lens_ref, lens_sem)
@@ -53,7 +53,7 @@
         return pltpu.make_async_remote_copy(
             src_ref=buf.at[h, src],
             dst_ref=buf.at[h, dst],
-            send_sem=ssem.at[h, s],
+            send_sem=ssem.at[s],
             recv_sem=rsem.at[h, r],
             device_id=device,
             device_id_type=MESH,
@@ -89,7 +89,10 @@
         to_left(h).start()
         to_right(h).start()
         to_across(h).start()
-        share(h, 4).start()
+
+        @pl.when(i == 1)
+        def _():
+            share(h, BACK).start()
 
     def stage2(h):
         for slot in (1, 3, 2):
@@ -117,21 +120,24 @@
         for h in range(KVH):
             own(h, 0, BACK).start()
             own(h, 1, BACK).start()
-        for h in range(KVH):
-            own(h, 0, BACK).wait()
-            own(h, 1, BACK).wait()
+        behind = buf.at[:, block(BACK)]
+        pltpu.make_async_copy(behind, behind, fill_sem).wait()
 
     pl.semaphore_wait(barrier, 4 + jnp.minimum(c // ROW, 1) + jnp.minimum((n - 1 - c) // ROW, 1))
     for h in range(KVH):
-        own(h, 0).wait()
-        own(h, 1).wait()
+        mine = buf.at[h, block(0)]
+        pltpu.make_async_copy(mine, mine, kv_sem.at[h]).wait()
 
         @pl.when(has_up)
         def _():
             to_up(h).start()
 
-    for h in range(KVH):
-        share(h, 0).start()
+
+    @pl.when(i == 0)
+    def _():
+        for h in range(KVH):
+            share(h, 0).start()
+
     q_copy.start()
 
     lens_copy.wait()
@@ -190,21 +196,27 @@
         def _():
             stage2(h + 1)
 
-        for slot in range(BACK + 1):
+        for slot in (1, 2, 3, BACK * (1 - i)):
             shared(h, slot)
         compute(h)
 
-    @pl.loop(0, KVH)
-    def _(h):
-        @pl.when(has_up)
-        def _():
-            to_up(h).wait_send()
-
-        to_right(h).wait_send()
-        to_left(h).wait_send()
-        to_across(h).wait_send()
-        for slot in range(BACK + 1):
-            share(h, slot).wait_send()
+    def all_sent(sem):
+        every = buf.at[:, block(0)]
+        pltpu.make_async_remote_copy(
+            src_ref=every,
+            dst_ref=every,
+            send_sem=ssem.at[sem],
+            recv_sem=rsem.at[0, 0],
+            device_id=partner,
+            device_id_type=MESH,
+        ).wait_send()
+
+    @pl.when(has_up)
+    def _():
+        all_sent(0)
+
+    for sem in (1, 2, 3, 5, 6, 7, 4 + BACK * i):
+        all_sent(sem)
 
 
 def per_device(queries, keys, values, doc_lengths):
@@ -226,8 +238,9 @@
             pltpu.VMEM((PAIR * T, T), jnp.float32),
             pltpu.SemaphoreType.DMA,
             pltpu.SemaphoreType.DMA,
-            pltpu.SemaphoreType.DMA((KVH, 4)),
-            pltpu.SemaphoreType.DMA((KVH, 10)),
+            pltpu.SemaphoreType.DMA,
+            pltpu.SemaphoreType.DMA((KVH,)),
+            pltpu.SemaphoreType.DMA((9,)),
             pltpu.SemaphoreType.DMA((KVH, 10)),
         ],
         compiler_params=pltpu.CompilerParams(collective_id=0, has_side_effects=True, vmem_limit_bytes=24 << 20),

time: 42.5 us -> 41.6 us (0.979)
  Pallas kernels: 41 us -> 40 us
    pallas_call x1, Pallas kernels: 41 us -> 40 us  [per_device(): pl.pallas_call(kernel, out_shape=jax.ShapeDtypeStruct(queries.shape, quer...]
where the time goes in v4:
time: 41.6 us; the launch traced here: 41.4 us
  Pallas kernels  40 us (96%)
  local copies, waits for them, and re-layouts  1.32 us (3%)
    pallas_call x1, Pallas kernels, per_device(): pl.pallas_call(kernel, out_shape=jax.ShapeDtypeStruct(queries.shape, quer...  40 us
    unnamed x1, local copies, waits for them, and re-layouts  1.32 us

profile of v4, /device:TPU:256, one launch (start us, length us, event | category | flops | bytes accessed | tf_op | source)
XLA Modules:
  0.0 41.4 jit_solution(17073857261257657965)
XLA Ops:
  0.0 40.0 %shard_map.46 = bf16[128,8192]{1,0:T(8,128)(2,1)S(1)} custom-call(s32[1,192]{1,0:T(1,128)} %bitcast.1, bf16[128,8192]{1,0:T(8,128)(2,1)} %q_hbm.1, bf16[128,1024]{1,0:T(8,128)(2,1)} %k_hbm.1, bf16[128,1024]{1,0:T(8,128)(2,1)} %v_hbm.1), custom_call_target="tpu_custom_call" | custom-call | tf_op jit(solution)/shard_map/pallas_call | solution.py:227
  40.0 1.3 %copy.6 = bf16[128,8192]{1,0:T(8,128)(2,1)} copy(bf16[128,8192]{1,0:T(8,128)(2,1)S(1)} %shard_map.46) | data formatting | bytes 4194304

commit v5 on v4

--- a/solution.py
+++ b/solution.py
@@ -99,21 +99,22 @@
             arrived(h, slot)
             share(h, slot).start()
 
+    barrier = pltpu.get_barrier_semaphore()
+    for device in (left, right, across, partner):
+        pl.semaphore_signal(barrier, inc=1, device_id=device, device_id_type=MESH)
+
+    @pl.when(has_down)
+    def _():
+        pl.semaphore_signal(barrier, inc=1, device_id=down, device_id_type=MESH)
+
+    @pl.when(has_up)
+    def _():
+        pl.semaphore_signal(barrier, inc=1, device_id=up, device_id_type=MESH)
+
     for h in range(KVH):
         own(h, 0).start()
         own(h, 1).start()
     lens_copy.start()
-    barrier = pltpu.get_barrier_semaphore()
-    for device in (left, right, across, partner):
-        pl.semaphore_signal(barrier, inc=1, device_id=device, device_id_type=MESH)
-
-    @pl.when(has_down)
-    def _():
-        pl.semaphore_signal(barrier, inc=1, device_id=down, device_id_type=MESH)
-
-    @pl.when(has_up)
-    def _():
-        pl.semaphore_signal(barrier, inc=1, device_id=up, device_id_type=MESH)
 
     @pl.when(c < ROW)
     def _():

time: 41.6 us -> 41.6 us (level)
  no operation moved by 1% of the time
where the time goes in v5:
time: 41.6 us; the launch traced here: 41.3 us
  Pallas kernels  40 us (96%)
  local copies, waits for them, and re-layouts  1.32 us (3%)
    pallas_call x1, Pallas kernels, per_device(): pl.pallas_call(kernel, out_shape=jax.ShapeDtypeStruct(queries.shape, quer...  40 us
    unnamed x1, local copies, waits for them, and re-layouts  1.32 us

profile of v5, /device:TPU:256, one launch (start us, length us, event | category | flops | bytes accessed | tf_op | source)
XLA Modules:
  0.0 41.3 jit_solution(4779566846164919313)
XLA Ops:
  0.0 40.0 %shard_map.46 = bf16[128,8192]{1,0:T(8,128)(2,1)S(1)} custom-call(s32[1,192]{1,0:T(1,128)} %bitcast.1, bf16[128,8192]{1,0:T(8,128)(2,1)} %q_hbm.1, bf16[128,1024]{1,0:T(8,128)(2,1)} %k_hbm.1, bf16[128,1024]{1,0:T(8,128)(2,1)} %v_hbm.1), custom_call_target="tpu_custom_call" | custom-call | tf_op jit(solution)/shard_map/pallas_call | solution.py:228
  40.0 1.3 %copy.6 = bf16[128,8192]{1,0:T(8,128)(2,1)} copy(bf16[128,8192]{1,0:T(8,128)(2,1)S(1)} %shard_map.46) | data formatting | bytes 4194304
